TPU v7x, 128 devices: a whole 4x4x4 slice. The times are simulated.
128 devices in a mesh: sample: 8 (over y_hi, z), landmark: 16 (over y_lo, x, core).
Axes of the slice: x: 4, y: 4 (y_hi: 2, y_lo: 2; y = y_hi * 2 + y_lo), z: 4, core: 2. Of those that a mesh axis runs over, the one named last changes fastest.
Arguments:
- embeddings: bfloat16 [8192, 4096], P('sample'), may hold values from -6 to 6
- landmarks: bfloat16 [16384, 4096], P('landmark'), may hold values from -6 to 6
- factor: bfloat16 [16384, 16384], P('landmark', 'sample')
- flips: int32 [512, 8192], P(None, 'sample'), may hold values from 0 to 1
- labels: int32 [8192], P('sample'), may hold values from 0 to 1, as said below
- counts: int32 [8], replicated, may hold values from 256 to 1024, as said below
Outputs:
- whitened: bfloat16 [16384, 512], P(('sample', 'landmark'))
- statistic: float32 [512], replicated
Inputs may be any that keep to these rules, and one draw needn't show every extreme that they name: `counts`: one slab holds exactly 1024 live rows. `labels`: 0 or 1; the first slot of every slab is of corpus 0 and the second of corpus 1.
All inputs are finite; a program needn't handle non-finite values.
Results may differ from a plain program's by a relative error of at most 0.029.
Values may be sent and summed in bfloat16 or wider, within the bound.
A program may use at most 128 MiB of HBM per device.

v0:
```python
import math
import jax
import jax.numpy as jnp
from jax import lax
from jax.sharding import PartitionSpec as P

D = 4096
LANDMARKS = 16384


def whiten_maker(factor, moments_half):
    return lax.dot_general(
        factor, moments_half, (((0,), (1,)), ((), ())), preferred_element_type=jnp.float32
    )


def local(embeddings, landmarks, factor, flips, labels, counts):
    slot_count = embeddings.shape[0]
    slab_total = counts.shape[0]
    here_index = lax.axis_index("sample")
    own_count = jnp.sum(jnp.where(jnp.arange(slab_total, dtype=jnp.int32) == here_index, counts, 0))
    live_rows = (jnp.arange(slot_count, dtype=jnp.int32) < own_count).astype(jnp.float32)
    corpus = labels.astype(jnp.float32)
    count_a, count_b = lax.psum(
        (jnp.sum(live_rows * (1.0 - corpus)), jnp.sum(live_rows * corpus)), "sample"
    )
    balance = jnp.sqrt(count_a * count_b / (count_a + count_b))
    row_weight = live_rows * ((1.0 - corpus) / count_a - corpus / count_b) * balance
    wide_x = embeddings.astype(jnp.float32)
    row_scale = lax.rsqrt(jnp.mean(wide_x * wide_x, axis=1) + 1e-06)
    wide_z = landmarks.astype(jnp.float32)
    point_scale = lax.rsqrt(jnp.mean(wide_z * wide_z, axis=1) + 1e-06)
    signs = (2 * flips - 1).astype(jnp.bfloat16)
    cross = lax.dot_general(
        embeddings, landmarks, (((1,), (1,)), ((), ())), preferred_element_type=jnp.float32
    )
    kern = jnp.exp(0.5 * cross * row_scale[:, None] * point_scale[None, :] / math.sqrt(D))
    weighted = (row_weight[:, None] * kern).astype(jnp.bfloat16)
    partial_value = jnp.dot(signs, weighted, preferred_element_type=jnp.float32)
    summed = lax.psum(partial_value.astype(jnp.bfloat16), "sample")
    wide = lax.psum_scatter(
        whiten_maker(factor, summed).astype(jnp.bfloat16),
        "landmark",
        scatter_dimension=0,
        tiled=True,
    ).astype(jnp.float32)
    share = jnp.sum(wide * wide, axis=0)
    statistic = lax.psum(share, ("sample", "landmark")) / LANDMARKS
    return (wide.astype(jnp.bfloat16), statistic)


def solution(mesh):
    return jax.shard_map(
        local,
        mesh=mesh,
        in_specs=(
            P("sample", None),
            P("landmark", None),
            P("landmark", "sample"),
            P(None, "sample"),
            P("sample"),
            P(),
        ),
        out_specs=(P(("sample", "landmark"), None), P()),
        check_vma=False,
    )
```

profile of v0, /device:TPU:1, one launch (start us, length us, event | category | flops | bytes accessed | tf_op | source)
XLA Modules:
  0.0 293.1 jit_solution(10554155324927165992)
XLA Ops:
  7.2 0.0 all-reduce.3.cloned.1.call-start
  7.2 1.3 fusion.9
  8.5 2.0 select_reduce_fusion
  10.5 23.3 %all-reduce = (f32[]{:T(128)}, f32[]{:T(128)}) all-reduce(f32[]{:T(128)} %get-tuple-element.7, f32[]{:T(128)} %get-tuple-element.6), channel_id=1, replica_groups=mesh['sample'=8,'landmark'=16] {'sample'}, use_global_device_ids=true, to_apply=%region_2.3 | all-reduce | flops 2 | bytes 16 | tf_op jit(solution)/shard_map/psum | solution.py:24
  36.3 2.5 select_multiply_fusion
  38.9 0.0 copy-start
  38.9 5.2 %multiply_reduce_fusion.1 = f32[1024]{0:T(1024)S(1)} fusion(bf16[1024,4096]{1,0:T(8,128)(2,1)} %param.6), kind=kLoop, calls=%fused_computation.1 | loop fusion | flops 12581888 | bytes 8392704 | tf_op jit(solution)/shard_map/reduce_sum | solution.py:30
  44.1 0.5 copy-done
  44.7 0.0 copy-start.1
  44.7 1.7 multiply_reduce_fusion
  46.4 0.0 copy-done.1
  46.4 16.2 %fusion.6 = bf16[512,1024]{1,0:T(8,128)(2,1)} fusion(bf16[1024,4096]{1,0:T(8,128)(2,1)} %param.6, bf16[1024,4096]{1,0:T(8,128)(2,1)} %param.7, f32[1024]{0:T(1024)S(1)} %get-tuple-element.10, f32[1024]{0:T(1024)S(1)} %get-tuple-element.11, f32[1024]{0:T(1024)S(1)} %select_multiply_fusion, s32[512,1024]{1,0:T(8,128)S(1)} %copy-done.1), kind=kOutput, calls=%fused_computation.11 | convolution fusion | flops 9671016448 | bytes 19935232 | tf_op jit(solution)/shard_map/dot_general | solution.py:39
  62.6 0.0 all-reduce.3.cloned.1.call-update
  62.6 0.0 reduce-scatter.4.cloned.1.call-start
  62.7 83.6 %all-reduce.3.cloned.1.call-done = bf16[512,1024]{1,0:T(8,128)(2,1)} async-done(((bf16[512,1024]{1,0:T(8,128)(2,1)}), bf16[512,1024]{1,0:T(8,128)(2,1)}) %all-reduce.3.cloned.1.call-update) | async-done | bytes 1048592 | tf_op jit(solution)/shard_map/psum | solution.py:40
  146.3 4.8 %fusion = bf16[2048,512]{0,1:T(8,128)(2,1)S(1)} fusion(bf16[512,1024]{1,0:T(8,128)(2,1)} %all-reduce.3.cloned.1.call-done, bf16[1024,2048]{1,0:T(8,128)(2,1)} %param.8), kind=kOutput, calls=%fused_computation.4 | convolution fusion | flops 2148532224 | bytes 7340032 | tf_op jit(solution)/shard_map/dot_general | solution.py:12
  151.1 2.5 copy.10
  153.6 0.0 reduce-scatter.4.cloned.1.call-update
  153.7 62.8 %reduce-scatter.4.cloned.1.call-done = bf16[128,512]{1,0:T(8,128)(2,1)} async-done(((bf16[2048,512]{1,0:T(8,128)(2,1)}), bf16[128,512]{1,0:T(8,128)(2,1)}) %reduce-scatter.4.cloned.1.call-update) | async-done | bytes 131088
  216.4 1.0 copy.11
  217.4 0.2 multiply_reduce_fusion.2
  217.6 68.1 %psum.31 = f32[512]{0:T(512)S(1)} all-reduce(f32[512]{0:T(512)S(1)} %multiply_reduce_fusion.2), channel_id=1, replica_groups=mesh['sample'=8,'landmark'=16] {'sample','landmark'}, use_global_device_ids=true, to_apply=%region_10.11 | all-reduce | flops 512 | bytes 4096 | tf_op jit(solution)/shard_map/psum | solution.py:48
  285.7 0.6 broadcast_multiply_fusion
  (1 shorter events, 0.0 us)
Async XLA Ops:
  7.2 139.1 %all-reduce.3.cloned.1.call-start = ((), (), s32[]{:S(2)}) async-start(), calls=%async_computation.1 | async-start | bytes 2097152 | tf_op jit(solution)/shard_map/psum | solution.py:40
  38.9 5.8 %copy-start = (bf16[1024,4096]{1,0:T(8,128)(2,1)S(1)}, bf16[1024,4096]{1,0:T(8,128)(2,1)}, u32[]{:S(2)}) copy-start(bf16[1024,4096]{1,0:T(8,128)(2,1)} %param.7) | copy-start | bytes 25165828
  44.7 1.7 copy-start.1
  62.6 153.8 %reduce-scatter.4.cloned.1.call-start = ((), (), s32[]{:S(2)}) async-start(), calls=%async_computation.2 | async-start | bytes 2228224
Sparse Core Ops, SparseCore 0:
  62.7 83.4 all-reduce.2
  153.8 62.5 reduce-scatter.3
where the time goes:
time: 293 us
  waiting for transfers between devices  146 us (50%)
  blocking collectives  91.4 us (31%)
  matrix products  21.1 us (7%)
  between operations  16.6 us (6%)
  other arithmetic  13.5 us (5%)
  local copies, waits for them, and re-layouts  4.09 us (1%)
    psum x1, waiting for transfers between devices, local(): summed = lax.psum(partial_value.astype(jnp.bfloat16), 'sample')  83.6 us
    psum x1, blocking collectives, local(): statistic = lax.psum(share, ('sample', 'landmark')) / LANDMARKS  68.1 us
    unnamed x3, waiting for transfers between devices  62.8 us
    psum x1, blocking collectives, local(): lax.psum((jnp.sum(live_rows * (1.0 - corpus)), jnp.sum(live_rows * corpus...  23.3 us
    dot_general x1, matrix products, local(): partial_value = jnp.dot(signs, weighted, preferred_element_type=jnp.float32)  16.2 us
  transfers between devices with their start and end apart: 2, of which 2 were waited for; matrix products, arithmetic and copies ran while one was open for 0% of the time, Pallas kernels for 0%

commit v1 on v0

--- a/solution.py
+++ b/solution.py
@@ -6,6 +6,12 @@
 
 D = 4096
 LANDMARKS = 16384
+
+
+def add_all(x, axis):
+    pieces = lax.all_gather(x, axis, axis=0, tiled=False)
+    summed = pieces.sum(axis=0)
+    return summed
 
 
 def whiten_maker(factor, moments_half):
@@ -37,7 +43,7 @@
     kern = jnp.exp(0.5 * cross * row_scale[:, None] * point_scale[None, :] / math.sqrt(D))
     weighted = (row_weight[:, None] * kern).astype(jnp.bfloat16)
     partial_value = jnp.dot(signs, weighted, preferred_element_type=jnp.float32)
-    summed = lax.psum(partial_value.astype(jnp.bfloat16), "sample")
+    summed = add_all(partial_value.astype(jnp.bfloat16), "sample")
     wide = lax.psum_scatter(
         whiten_maker(factor, summed).astype(jnp.bfloat16),
         "landmark",

time: 293 us -> 318 us (1.085)
  waiting for transfers between devices: 146 us -> 165 us
  other arithmetic: 13.5 us -> 19.2 us
    all_gather x0 -> x1, waiting for transfers between devices: none -> 107 us  [add_all(): pieces = lax.all_gather(x, axis, axis=0, tiled=False)]
    psum x1 -> x0, waiting for transfers between devices: 83.6 us -> none  [local(): summed = lax.psum(partial_value.astype(jnp.bfloat16), 'sample')]
    reduce_sum x0 -> x1, other arithmetic: none -> 5.66 us  [add_all(): summed = pieces.sum(axis=0)]
    unnamed x3, waiting for transfers between devices: 62.8 us -> 57.8 us
where the time goes in v1:
time: 318 us
  waiting for transfers between devices  165 us (52%)
  blocking collectives  91.7 us (29%)
  matrix products  20.7 us (7%)
  other arithmetic  19.2 us (6%)
  between operations  16.6 us (5%)
  local copies, waits for them, and re-layouts  4.09 us (1%)
    all_gather x1, waiting for transfers between devices, add_all(): pieces = lax.all_gather(x, axis, axis=0, tiled=False)  107 us
    psum x1, blocking collectives, local(): statistic = lax.psum(share, ('sample', 'landmark')) / LANDMARKS  68.4 us
    unnamed x3, waiting for transfers between devices  57.8 us
    psum x1, blocking collectives, local(): lax.psum((jnp.sum(live_rows * (1.0 - corpus)), jnp.sum(live_rows * corpus...  23.3 us
    dot_general x1, matrix products, local(): partial_value = jnp.dot(signs, weighted, preferred_element_type=jnp.float32)  16.2 us
  transfers between devices with their start and end apart: 2, of which 2 were waited for; matrix products, arithmetic and copies ran while one was open for 0% of the time, Pallas kernels for 0%

profile of v1, /device:TPU:1, one launch (start us, length us, event | category | flops | bytes accessed | tf_op | source)
XLA Modules:
  0.0 317.7 jit_solution(42927059822604455)
XLA Ops:
  7.2 0.0 all-gather.3.cloned.1.call-start
  7.2 1.3 fusion.9
  8.5 2.0 select_reduce_fusion
  10.5 23.3 %all-reduce = (f32[]{:T(128)}, f32[]{:T(128)}) all-reduce(f32[]{:T(128)} %get-tuple-element.7, f32[]{:T(128)} %get-tuple-element.6), channel_id=1, replica_groups=mesh['sample'=8,'landmark'=16] {'sample'}, use_global_device_ids=true, to_apply=%region_2.3 | all-reduce | flops 2 | bytes 16 | tf_op jit(solution)/shard_map/psum | solution.py:30
  36.3 2.5 select_multiply_fusion
  38.9 0.0 copy-start
  38.9 5.2 %multiply_reduce_fusion.1 = f32[1024]{0:T(1024)S(1)} fusion(bf16[1024,4096]{1,0:T(8,128)(2,1)} %param.6), kind=kLoop, calls=%fused_computation.1 | loop fusion | flops 12581888 | bytes 8392704 | tf_op jit(solution)/shard_map/reduce_sum | solution.py:36
  44.1 0.5 copy-done
  44.7 0.0 copy-start.1
  44.7 1.7 multiply_reduce_fusion
  46.4 0.0 copy-done.1
  46.4 16.2 %fusion.6 = bf16[512,1024]{1,0:T(8,128)(2,1)} fusion(bf16[1024,4096]{1,0:T(8,128)(2,1)} %param.6, bf16[1024,4096]{1,0:T(8,128)(2,1)} %param.7, f32[1024]{0:T(1024)S(1)} %get-tuple-element.10, f32[1024]{0:T(1024)S(1)} %get-tuple-element.11, f32[1024]{0:T(1024)S(1)} %select_multiply_fusion, s32[512,1024]{1,0:T(8,128)S(1)} %copy-done.1), kind=kOutput, calls=%fused_computation.11 | convolution fusion | flops 9671016448 | bytes 19935232 | tf_op jit(solution)/shard_map/dot_general | solution.py:45
  62.6 0.0 all-gather.3.cloned.1.call-update
  62.6 0.2 reduce-scatter.4.cloned.1.call-start
  62.8 107.3 %all-gather.3.cloned.1.call-done = bf16[4096,1024]{1,0:T(8,128)(2,1)} async-done(((bf16[512,1024]{1,0:T(8,128)(2,1)}), bf16[4096,1024]{1,0:T(8,128)(2,1)}) %all-gather.3.cloned.1.call-update) | async-done | bytes 8388624 | tf_op jit(solution)/shard_map/all_gather | solution.py:12
  170.1 5.7 %reduce_sum.71 = bf16[512,1024]{1,0:T(8,128)(2,1)S(1)} reduce(bf16[8,512,1024]{2,1,0:T(8,128)(2,1)} %bitcast.8, bf16[]{:T(256)} %constant.34.clone.1), dimensions={0}, to_apply=%region_7.8 | reduce | flops 3670016 | bytes 9437186 | tf_op jit(solution)/shard_map/reduce_sum | solution.py:13
  175.8 4.5 %fusion = bf16[2048,512]{0,1:T(8,128)(2,1)S(1)} fusion(bf16[512,1024]{1,0:T(8,128)(2,1)S(1)} %reduce_sum.71, bf16[1024,2048]{1,0:T(8,128)(2,1)} %param.8), kind=kOutput, calls=%fused_computation.4 | convolution fusion | flops 2148532224 | bytes 7340032 | tf_op jit(solution)/shard_map/dot_general | solution.py:18
  180.3 2.5 copy.10
  182.9 0.0 reduce-scatter.4.cloned.1.call-update
  182.9 57.8 %reduce-scatter.4.cloned.1.call-done = bf16[128,512]{1,0:T(8,128)(2,1)} async-done(((bf16[2048,512]{1,0:T(8,128)(2,1)}), bf16[128,512]{1,0:T(8,128)(2,1)}) %reduce-scatter.4.cloned.1.call-update) | async-done | bytes 131088
  240.7 1.0 copy.11
  241.7 0.2 multiply_reduce_fusion.2
  241.8 68.4 %psum.23 = f32[512]{0:T(512)S(1)} all-reduce(f32[512]{0:T(512)S(1)} %multiply_reduce_fusion.2), channel_id=1, replica_groups=mesh['sample'=8,'landmark'=16] {'sample','landmark'}, use_global_device_ids=true, to_apply=%region_10.11 | all-reduce | flops 512 | bytes 4096 | tf_op jit(solution)/shard_map/psum | solution.py:54
  310.2 0.6 broadcast_multiply_fusion
  (1 shorter events, 0.0 us)
Async XLA Ops:
  7.2 163.0 %all-gather.3.cloned.1.call-start = ((), (), s32[]{:S(2)}) async-start(), calls=%async_computation.1 | async-start | bytes 9437184 | tf_op jit(solution)/shard_map/all_gather | solution.py:12
  38.9 5.8 %copy-start = (bf16[1024,4096]{1,0:T(8,128)(2,1)S(1)}, bf16[1024,4096]{1,0:T(8,128)(2,1)}, u32[]{:S(2)}) copy-start(bf16[1024,4096]{1,0:T(8,128)(2,1)} %param.7) | copy-start | bytes 25165828
  44.7 1.7 copy-start.1
  62.6 178.1 %reduce-scatter.4.cloned.1.call-start = ((), (), s32[]{:S(2)}) async-start(), calls=%async_computation.2 | async-start | bytes 2228224
Sparse Core Ops, SparseCore 0:
  62.7 107.3 all-gather.2
  183.0 57.5 reduce-scatter.3

commit v2 on v0

--- a/solution.py
+++ b/solution.py
@@ -6,6 +6,11 @@
 
 D = 4096
 LANDMARKS = 16384
+
+
+def by_each_axis(array, inner_axis, outer_axis):
+    half = lax.psum(array, inner_axis)
+    return lax.psum(half, outer_axis)
 
 
 def whiten_maker(factor, moments_half):
@@ -45,7 +50,7 @@
         tiled=True,
     ).astype(jnp.float32)
     share = jnp.sum(wide * wide, axis=0)
-    statistic = lax.psum(share, ("sample", "landmark")) / LANDMARKS
+    statistic = by_each_axis(share, "sample", "landmark") / LANDMARKS
     return (wide.astype(jnp.bfloat16), statistic)
 
 

time: 293 us -> 280 us (0.956)
  blocking collectives: 91.4 us -> 78.2 us
    psum x1 -> x2, blocking collectives: 68.1 us -> 54.9 us  [the longest x1 34.2 us: by_each_axis(): return lax.psum(half, outer_axis)]
where the time goes in v2:
time: 280 us
  waiting for transfers between devices  146 us (52%)
  blocking collectives  78.2 us (28%)
  matrix products  21.1 us (8%)
  between operations  16.6 us (6%)
  other arithmetic  13.5 us (5%)
  local copies, waits for them, and re-layouts  4.09 us (1%)
    psum x1, waiting for transfers between devices, local(): summed = lax.psum(partial_value.astype(jnp.bfloat16), 'sample')  83.6 us
    unnamed x3, waiting for transfers between devices  62.8 us
    psum x1, blocking collectives, by_each_axis(): return lax.psum(half, outer_axis)  34.2 us
    psum x1, blocking collectives, local(): lax.psum((jnp.sum(live_rows * (1.0 - corpus)), jnp.sum(live_rows * corpus...  23.3 us
    psum x1, blocking collectives, by_each_axis(): half = lax.psum(array, inner_axis)  20.7 us
    dot_general x1, matrix products, local(): partial_value = jnp.dot(signs, weighted, preferred_element_type=jnp.float32)  16.2 us
  transfers between devices with their start and end apart: 2, of which 2 were waited for; matrix products, arithmetic and copies ran while one was open for 0% of the time, Pallas kernels for 0%

profile of v2, /device:TPU:1, one launch (start us, length us, event | category | flops | bytes accessed | tf_op | source)
XLA Modules:
  0.0 279.9 jit_solution(16586349000923222312)
XLA Ops:
  7.2 0.0 all-reduce.3.cloned.1.call-start
  7.2 1.3 fusion.9
  8.5 2.0 select_reduce_fusion
  10.5 23.3 %all-reduce = (f32[]{:T(128)}, f32[]{:T(128)}) all-reduce(f32[]{:T(128)} %get-tuple-element.7, f32[]{:T(128)} %get-tuple-element.6), channel_id=1, replica_groups=mesh['sample'=8,'landmark'=16] {'sample'}, use_global_device_ids=true, to_apply=%region_2.3 | all-reduce | flops 2 | bytes 16 | tf_op jit(solution)/shard_map/psum | solution.py:29
  36.3 2.5 select_multiply_fusion
  38.9 0.0 copy-start
  38.9 5.2 %multiply_reduce_fusion.1 = f32[1024]{0:T(1024)S(1)} fusion(bf16[1024,4096]{1,0:T(8,128)(2,1)} %param.6), kind=kLoop, calls=%fused_computation.1 | loop fusion | flops 12581888 | bytes 8392704 | tf_op jit(solution)/shard_map/reduce_sum | solution.py:35
  44.1 0.5 copy-done
  44.7 0.0 copy-start.1
  44.7 1.7 multiply_reduce_fusion
  46.4 0.0 copy-done.1
  46.4 16.2 %fusion.6 = bf16[512,1024]{1,0:T(8,128)(2,1)} fusion(bf16[1024,4096]{1,0:T(8,128)(2,1)} %param.6, bf16[1024,4096]{1,0:T(8,128)(2,1)} %param.7, f32[1024]{0:T(1024)S(1)} %get-tuple-element.10, f32[1024]{0:T(1024)S(1)} %get-tuple-element.11, f32[1024]{0:T(1024)S(1)} %select_multiply_fusion, s32[512,1024]{1,0:T(8,128)S(1)} %copy-done.1), kind=kOutput, calls=%fused_computation.11 | convolution fusion | flops 9671016448 | bytes 19935232 | tf_op jit(solution)/shard_map/dot_general | solution.py:44
  62.6 0.0 all-reduce.3.cloned.1.call-update
  62.6 0.0 reduce-scatter.4.cloned.1.call-start
  62.7 83.6 %all-reduce.3.cloned.1.call-done = bf16[512,1024]{1,0:T(8,128)(2,1)} async-done(((bf16[512,1024]{1,0:T(8,128)(2,1)}), bf16[512,1024]{1,0:T(8,128)(2,1)}) %all-reduce.3.cloned.1.call-update) | async-done | bytes 1048592 | tf_op jit(solution)/shard_map/psum | solution.py:45
  146.3 4.8 %fusion = bf16[2048,512]{0,1:T(8,128)(2,1)S(1)} fusion(bf16[512,1024]{1,0:T(8,128)(2,1)} %all-reduce.3.cloned.1.call-done, bf16[1024,2048]{1,0:T(8,128)(2,1)} %param.8), kind=kOutput, calls=%fused_computation.4 | convolution fusion | flops 2148532224 | bytes 7340032 | tf_op jit(solution)/shard_map/dot_general | solution.py:17
  151.1 2.5 copy.10
  153.6 0.0 reduce-scatter.4.cloned.1.call-update
  153.7 62.8 %reduce-scatter.4.cloned.1.call-done = bf16[128,512]{1,0:T(8,128)(2,1)} async-done(((bf16[2048,512]{1,0:T(8,128)(2,1)}), bf16[128,512]{1,0:T(8,128)(2,1)}) %reduce-scatter.4.cloned.1.call-update) | async-done | bytes 131088
  216.4 1.0 copy.11
  217.4 0.2 multiply_reduce_fusion.2
  217.6 20.7 %psum.38 = f32[512]{0:T(512)S(1)} all-reduce(f32[512]{0:T(512)S(1)} %multiply_reduce_fusion.2), channel_id=1, replica_groups=mesh['sample'=8,'landmark'=16] {'sample'}, use_global_device_ids=true, to_apply=%region_10.11 | all-reduce | flops 512 | bytes 4096 | tf_op jit(solution)/shard_map/psum | solution.py:12
  238.3 34.2 %psum.39 = f32[512]{0:T(512)S(1)} all-reduce(f32[512]{0:T(512)S(1)} %psum.38), channel_id=1, replica_groups=mesh['sample'=8,'landmark'=16] {'landmark'}, use_global_device_ids=true, to_apply=%region_11.12 | all-reduce | flops 512 | bytes 4096 | tf_op jit(solution)/shard_map/psum | solution.py:13
  272.4 0.6 broadcast_multiply_fusion
  (1 shorter events, 0.0 us)
Async XLA Ops:
  7.2 139.1 %all-reduce.3.cloned.1.call-start = ((), (), s32[]{:S(2)}) async-start(), calls=%async_computation.1 | async-start | bytes 2097152 | tf_op jit(solution)/shard_map/psum | solution.py:45
  38.9 5.8 %copy-start = (bf16[1024,4096]{1,0:T(8,128)(2,1)S(1)}, bf16[1024,4096]{1,0:T(8,128)(2,1)}, u32[]{:S(2)}) copy-start(bf16[1024,4096]{1,0:T(8,128)(2,1)} %param.7) | copy-start | bytes 25165828
  44.7 1.7 copy-start.1
  62.6 153.8 %reduce-scatter.4.cloned.1.call-start = ((), (), s32[]{:S(2)}) async-start(), calls=%async_computation.2 | async-start | bytes 2228224
Sparse Core Ops, SparseCore 0:
  62.7 83.4 all-reduce.2
  153.8 62.5 reduce-scatter.3
